TPU v7x, 128 devices: a whole 4x4x4 slice. The times are simulated.
128 devices in a mesh: req: 16 (over x, y), exp: 8 (over z, core).
Axes of the slice: x: 4, y: 4, z: 4, core: 2. Of those that a mesh axis runs over, the one named last changes fastest.
Arguments:
- tokens: bfloat16 [16384, 2048], P(('req', 'exp')), may hold values from -6 to 6
- attn_gain: float32 [2048], replicated, may hold values from 0.1 to 1.9
- w_query: bfloat16 [2048, 2048], P(None, 'exp'), may hold values from -0.25 to 0.25
- w_key: bfloat16 [2048, 2048], P(None, 'exp'), may hold values from -0.125 to 0.125
- w_value: bfloat16 [2048, 2048], P(None, 'exp'), may hold values from -0.125 to 0.125
- w_out: bfloat16 [2048, 2048], P('exp'), may hold values from -0.375 to 0.375
- prefix_cache: bfloat16 [8, 1024, 2, 2048], P(None, 'req', None, 'exp'), may hold values from -205 to 205
- group_of: int32 [16], replicated, may hold values from 0 to 7
- lengths: int32 [16], replicated, may hold values from 1 to 1024, 10240 in all
- moe_gain: float32 [2048], replicated, may hold values from 0.1 to 1.9
- w_gate: bfloat16 [128, 2048, 512], P(('req', 'exp')), may hold values from -0.125 to 0.125
- w_up: bfloat16 [128, 2048, 512], P(('req', 'exp')), may hold values from -0.125 to 0.125
- w_down: bfloat16 [128, 512, 2048], P(('req', 'exp')), may hold values from -0.25 to 0.25
- routes: int32 [16384, 8], P(('req', 'exp')), may hold values from 0 to 63, all different within a row; in each aligned block of 128 rows (0 to 127, 128 to 255, ...) at most 18 rows name the same one
- route_weights: float32 [16384, 8], P(('req', 'exp')), may hold values from 0.1 to 0.4
Outputs:
- layer_out: bfloat16 [16384, 2048], P(('req', 'exp'))
Inputs may be any that keep to these rules, and one draw needn't show every extreme that they name: `routes`: in the rows of one device no expert is named more than 18 times.
All inputs are finite; a program needn't handle non-finite values.
Results may differ from a plain program's by a relative error of at most 0.017.
Values may be sent and summed in bfloat16 or wider, within the bound.
No kernel may reach another device: no remote copies, remote signals or barrier semaphores. Data moves between devices by JAX's collectives and lax.ppermute only.
A program may use at most 192 MiB of HBM per device.

v0:
```python
import math
import jax
import jax.numpy as jnp
from jax import lax
from jax.sharding import PartitionSpec as P

HD = 128
PREFIX = 1024


def norm_rows(values, gain):
    wide = values.astype(jnp.float32)
    return wide * lax.rsqrt(jnp.mean(wide * wide, axis=-1, keepdims=True) + 1e-05) * gain


def rotate(vectors, places):
    half = vectors.shape[-1] // 2
    freqs = 10000.0 ** (-(jnp.arange(half, dtype=jnp.float32) * 2.0) / vectors.shape[-1])
    angles = places[:, None] * freqs[None, :]
    cosine = jnp.cos(angles)[:, None, :]
    sine = jnp.sin(angles)[:, None, :]
    first = vectors[..., :half]
    second = vectors[..., half:]
    return jnp.concatenate(
        [first * cosine - second * sine, first * sine + second * cosine], axis=-1
    )


def on_device(
    tokens,
    attn_gain,
    w_query,
    w_key,
    w_value,
    w_out,
    prefix_cache,
    group_of,
    lengths,
    moe_gain,
    w_gate,
    w_up,
    w_down,
    routes,
    route_weights,
):
    rows_dev, width = tokens.shape
    exp_count = lax.axis_size("exp")
    req_count = lax.axis_size("req")
    exp_index = lax.axis_index("exp")
    req_index = lax.axis_index("req")
    local_width = w_query.shape[1]
    head_dim = HD
    local_heads = local_width // head_dim
    slot_count = rows_dev * exp_count
    normed = norm_rows(tokens, attn_gain).astype(jnp.bfloat16)
    joined = jnp.concatenate([w_query, w_key, w_value], axis=1)
    piece = lax.all_gather(normed, "exp", axis=0, tiled=True)
    count = piece.shape[0]
    mixed = jnp.dot(piece, joined, preferred_element_type=jnp.float32)
    places = (PREFIX + jnp.int32(0) + jnp.arange(count, dtype=jnp.int32)).astype(jnp.float32)
    query = rotate(mixed[:, :local_width].reshape(count, local_heads, head_dim), places).reshape(
        count, local_width
    )
    key = rotate(
        mixed[:, local_width : 2 * local_width].reshape(count, local_heads, head_dim), places
    ).reshape(count, local_width)
    projected = jnp.concatenate([query, key, mixed[:, 2 * local_width :]], axis=1).astype(
        jnp.bfloat16
    )
    outgoing = jnp.take(prefix_cache, group_of, axis=0)
    arrived = lax.all_to_all(outgoing, "req", split_axis=0, concat_axis=1, tiled=True)[0]
    prefix_len = arrived.shape[0]
    query = projected[:, :local_width].reshape(slot_count, local_heads, head_dim)
    keys = jnp.concatenate(
        [
            arrived[:, 0].reshape(prefix_len, local_heads, head_dim),
            projected[:, local_width : 2 * local_width].reshape(slot_count, local_heads, head_dim),
        ],
        axis=0,
    )
    values = jnp.concatenate(
        [
            arrived[:, 1].reshape(prefix_len, local_heads, head_dim),
            projected[:, 2 * local_width :].reshape(slot_count, local_heads, head_dim),
        ],
        axis=0,
    )
    scores = jnp.einsum(
        "qhd,khd->hqk", query, keys, preferred_element_type=jnp.float32
    ) / math.sqrt(head_dim)
    length = lengths[req_index]
    live = jnp.concatenate(
        [jnp.ones((prefix_len,), bool), jnp.arange(slot_count, dtype=jnp.int32) < length]
    )
    scores = jnp.where(live[None, None, :], scores, -1e30)
    top_score = jnp.max(scores, axis=-1, keepdims=True)
    raised = jnp.exp(scores - top_score)
    probs = (raised / jnp.sum(raised, axis=-1, keepdims=True)).astype(jnp.bfloat16)
    attn = (
        jnp.einsum("hqk,khd->qhd", probs, values, preferred_element_type=jnp.float32)
        .astype(jnp.bfloat16)
        .reshape(slot_count, local_width)
    )
    attn_out = lax.psum_scatter(
        jnp.dot(attn, w_out, preferred_element_type=jnp.float32).astype(jnp.bfloat16),
        "exp",
        scatter_dimension=0,
        tiled=True,
    ).astype(jnp.float32)
    hidden_state = (tokens.astype(jnp.float32) + attn_out).astype(jnp.bfloat16)
    normed2 = norm_rows(hidden_state, moe_gain).astype(jnp.bfloat16)
    top_count = routes.shape[1]
    experts = req_count * exp_count // 2
    capacity = 2 * max(1, rows_dev * top_count * 9 // (16 * experts))
    flat = routes.reshape(-1)
    onehot = (flat[:, None] == jnp.arange(experts, dtype=jnp.int32)[None, :]).astype(jnp.int32)
    slot = jnp.sum((jnp.cumsum(onehot, axis=0) - 1) * onehot, axis=1)
    source_row = jnp.arange(rows_dev * top_count, dtype=jnp.int32) // top_count
    buffer = (
        jnp.zeros((experts, capacity, width), jnp.bfloat16).at[flat, slot].set(normed2[source_row])
    )
    doubled = jnp.broadcast_to(buffer[:, None], (experts, 2, capacity, width)).reshape(
        2 * experts, capacity, width
    )
    rows_in = lax.all_to_all(doubled, ("req", "exp"), split_axis=0, concat_axis=0, tiled=True)
    senders, count, _ = rows_in.shape
    joined_rows = rows_in.reshape(senders * count, width)
    gate = jnp.dot(joined_rows, w_gate[0], preferred_element_type=jnp.float32)
    upper = jnp.dot(joined_rows, w_up[0], preferred_element_type=jnp.float32)
    act = (jax.nn.silu(gate) * upper).astype(jnp.bfloat16)
    part = jnp.dot(act, w_down[0], preferred_element_type=jnp.float32)
    returned = lax.all_to_all(
        part.reshape(senders, count, width).astype(jnp.bfloat16),
        ("req", "exp"),
        split_axis=0,
        concat_axis=0,
        tiled=True,
    ).astype(jnp.float32)
    combined = (
        jnp.sum(returned.reshape(experts, 2, capacity, width), axis=1)
        .astype(jnp.bfloat16)
        .astype(jnp.float32)
    )
    picked = combined[flat, slot].reshape(rows_dev, top_count, width)
    moe = jnp.sum(picked * route_weights[:, :, None], axis=1)
    place = exp_index * rows_dev + jnp.arange(rows_dev, dtype=jnp.int32)
    live_rows = place < length
    return jnp.where(live_rows[:, None], hidden_state.astype(jnp.float32) + moe, 0.0).astype(
        jnp.bfloat16
    )


def solution(mesh):
    return jax.shard_map(
        on_device,
        mesh=mesh,
        in_specs=(
            P(("req", "exp"), None),
            P(),
            P(None, "exp"),
            P(None, "exp"),
            P(None, "exp"),
            P("exp", None),
            P(None, "req", None, "exp"),
            P(),
            P(),
            P(),
            P(("req", "exp"), None, None),
            P(("req", "exp"), None, None),
            P(("req", "exp"), None, None),
            P(("req", "exp"), None),
            P(("req", "exp"), None),
        ),
        out_specs=P(("req", "exp"), None),
        check_vma=False,
    )
```

profile of v0, /device:TPU:24, one launch (start us, length us, event | category | flops | bytes accessed | tf_op | source)
XLA Modules:
  0.0 606.7 jit_solution(18141215170195101366)
XLA Ops:
  6.5 1.4 fusion.25
  7.9 2.0 fusion.27
  10.0 0.7 compare_select_fusion.3
  10.7 3.7 gather_fusion
  14.4 0.7 compare_and_fusion
  15.0 2.0 broadcast_select_fusion
  17.0 7.2 %all-to-all-start = ((bf16[16,64,2,256]{3,2,1,0:T(2,128)(2,1)}), bf16[16,64,2,256]{3,2,1,0:T(2,128)(2,1)S(1)}, u32[]{:S(2)}, u32[]{:S(2)}) async-start(bf16[16,64,2,256]{3,2,1,0:T(2,128)(2,1)} %broadcast_select_fusion), calls=%async_computation | async-start | bytes 2097152 | tf_op jit(solution)/shard_map/all_to_all | solution.py:71
  25.7 3.1 multiply_cosine_fusion
  28.8 10.1 %all-to-all-done = bf16[16,64,2,256]{3,2,1,0:T(2,128)(2,1)S(1)} async-done(((bf16[16,64,2,256]{3,2,1,0:T(2,128)(2,1)}), bf16[16,64,2,256]{3,2,1,0:T(2,128)(2,1)S(1)}, u32[]{:S(2)}, u32[]{:S(2)}) %all-to-all-start) | async-done | bytes 1048608 | tf_op jit(solution)/shard_map/all_to_all | solution.py:71
  39.1 0.9 fusion.50
  40.0 1.2 copy.89
  41.2 1.0 copy.92
  42.3 1.0 copy.86
  43.3 1.3 all-gather.2.cloned.1.call-done
  44.5 6.7 %fusion.10 = f32[1024,768]{0,1:T(8,128)S(1)} fusion(bf16[1024,2048]{1,0:T(8,128)(2,1)} %all-gather.2.cloned.1.call-done, bf16[2048,256]{1,0:T(8,128)(2,1)} %param.19, bf16[2048,256]{1,0:T(8,128)(2,1)} %param.18, bf16[2048,256]{1,0:T(8,128)(2,1)} %param.17), kind=kOutput, calls=%fused_computation.23 | convolution fusion | flops 3230662656 | bytes 10485760 | tf_op jit(solution)/shard_map/dot_general | solution.py:59
  51.2 1.2 fusion.49
  52.4 0.9 slice.68
  53.3 1.0 fusion.51
  54.3 1.4 copy.103
  55.7 2.4 copy.104
  58.1 2.3 fusion.52
  60.4 2.4 copy.105
  62.7 2.4 copy.106
  65.1 3.9 subtract_convert_fusion.1
  69.0 10.8 %fusion.53 = (f32[2,1024]{1,0:T(2,128)S(1)}, f32[2,1024,2048]{2,1,0:T(8,128)}) fusion(pred[2048]{0:T(1024)(128)(4,1)S(1)} %concatenate.28, bf16[1024,2,64]{2,0,1:T(8,128)(2,1)} %get-tuple-element.13, bf16[1024,2,64]{2,0,1:T(8,128)(2,1)} %get-tuple-element.14, bf16[1024,2,128]{2,0,1:T(8,128)(2,1)} %copy.92, bf16[1024,2,64]{2,0,1:T(8,128)(2,1)} %get-tuple-element.6, ...), kind=kOutput, calls=%fused_computation.105 | convolution fusion | flops 1094715392 | bytes 18360320 | tf_op jit(solution)/shard_map/sub | solution.py:97
  79.9 8.8 %fusion.24 = bf16[2,128,1024]{2,1,0:T(8,128)(2,1)S(1)} fusion(f32[2,1024,2048]{2,1,0:T(8,128)} %get-tuple-element.25, f32[2,1024]{1,0:T(2,128)S(1)} %get-tuple-element.24, bf16[1024,2,128]{0,2,1:T(8,128)(2,1)S(1)} %bitcast.62, bf16[1024,2,128]{0,2,1:T(8,128)(2,1)S(1)} %bitcast.61), kind=kOutput, calls=%fused_computation.43 | convolution fusion | flops 1084489728 | bytes 18358272 | tf_op jit(solution)/shard_map/hqk,khd->qhd/dot_general | solution.py:100
  88.7 3.2 convolution_convert_fusion.1
  92.4 18.0 %reduce-window.6 = s32[64,8,128]{2,1,0:T(8,128)S(1)} reduce-window(s32[64,8,128]{2,1,0:T(8,128)S(1)} %fusion.39, s32[]{:T(128)} %constant.39.clone.1), window={size=1x1x128 pad=0_0x0_0x127_0}, to_apply=%region_4.5 | reduce-window | flops 8323072 | bytes 524292 | tf_op jit(solution)/shard_map/reduce-window
  111.3 19.1 %reduce-scatter.2.cloned.1.call-done = bf16[128,2048]{1,0:T(8,128)(2,1)} async-done(((bf16[1024,2048]{1,0:T(8,128)(2,1)}), bf16[128,2048]{1,0:T(8,128)(2,1)}) %reduce-scatter.2.cloned.1.call-update) | async-done | bytes 524304 | tf_op jit(solution)/shard_map/reduce_scatter | solution.py:104
  130.4 1.3 fusion.29
  131.7 1.3 fusion.31
  133.0 23.0 %scatter_custom_fusion = bf16[1152,2048]{1,0:T(8,128)(2,1)} fusion(s32[1024]{0:T(1024)S(1)} %get-tuple-element.27, bf16[128,2048]{1,0:T(8,128)(2,1)S(1)} %fusion.31, s32[1024]{0:T(1024)S(1)} %get-tuple-element.26, bf16[]{:T(256)} %constant.82.clone.1), kind=kCustom, calls=%fused_computation.20 | custom fusion | bytes 4718594
  155.9 5.1 copy.98
  161.0 1.6 broadcast_in_dim.43
  162.6 150.4 %all_to_all.19 = bf16[128,18,2048]{2,1,0:T(8,128)(2,1)} all-to-all(bf16[128,18,2048]{2,1,0:T(8,128)(2,1)S(1)} %bitcast.53), channel_id=1, replica_groups=mesh['req'=16,'exp'=8] {'req','exp'}, dimensions={0} | all-to-all | bytes 18874368 | tf_op jit(solution)/shard_map/all_to_all | solution.py:125
  313.0 14.1 %reshape.246 = bf16[2304,2048]{1,0:T(8,128)(2,1)} reshape(bf16[128,18,2048]{2,1,0:T(8,128)(2,1)} %all_to_all.19) | data formatting | bytes 18874368 | tf_op jit(solution)/shard_map/reshape | solution.py:127
  327.0 8.6 %fusion.20 = f32[2304,512]{1,0:T(8,128)S(1)} fusion(bf16[2304,2048]{1,0:T(8,128)(2,1)} %reshape.246, bf16[1,2048,512]{2,1,0:T(8,128)(2,1)} %param.25), kind=kOutput, calls=%fused_computation.33 | convolution fusion | flops 4831838208 | bytes 16252928 | tf_op jit(solution)/shard_map/dot_general | solution.py:128
  335.7 7.1 %fusion.7 = bf16[2304,512]{1,0:T(8,128)(2,1)} fusion(bf16[2304,2048]{1,0:T(8,128)(2,1)S(1)} %copy-done.2, f32[2304,512]{1,0:T(8,128)S(1)} %fusion.20, bf16[1,2048,512]{2,1,0:T(8,128)(2,1)S(1)} %copy-done.12), kind=kOutput, calls=%fused_computation.19 | convolution fusion | flops 4838916096 | bytes 18612224 | tf_op jit(solution)/shard_map/dot_general | solution.py:129
  342.7 4.9 dot_general.29
  347.6 7.3 %convolution_convert_fusion = bf16[128,18,2048]{2,0,1:T(8,128)(2,1)S(1)} fusion(bf16[128,18,512]{2,1,0:T(8,128)(2,1)} %dot_general.29, bf16[1,512,2048]{2,1,0:T(8,128)(2,1)S(1)} %copy-done), kind=kOutput, calls=%fused_computation.16 | convolution fusion | flops 4836556800 | bytes 13893632 | tf_op jit(solution)/shard_map/dot_general | solution.py:131
  354.9 20.9 %copy.100 = bf16[128,18,2048]{2,1,0:T(8,128)(2,1)} copy(bf16[128,18,2048]{2,0,1:T(8,128)(2,1)S(1)} %convolution_convert_fusion) | data formatting | bytes 18874368 | tf_op jit(solution)/shard_map/convert_element_type | solution.py:133
  375.8 10.1 %all-to-all-start.2 = ((bf16[128,18,2048]{2,1,0:T(8,128)(2,1)}), bf16[128,18,2048]{2,1,0:T(8,128)(2,1)}, u32[]{:S(2)}, u32[]{:S(2)}) async-start(bf16[128,18,2048]{2,1,0:T(8,128)(2,1)} %copy.100), calls=%async_computation.3 | async-start | bytes 25165824 | tf_op jit(solution)/shard_map/all_to_all | solution.py:132
  386.7 164.7 %all-to-all-done.2 = bf16[128,18,2048]{2,1,0:T(8,128)(2,1)} async-done(((bf16[128,18,2048]{2,1,0:T(8,128)(2,1)}), bf16[128,18,2048]{2,1,0:T(8,128)(2,1)}, u32[]{:S(2)}, u32[]{:S(2)}) %all-to-all-start.2) | async-done | bytes 9437216 | tf_op jit(solution)/shard_map/all_to_all | solution.py:132
  551.4 8.9 %bitcast_reduce_fusion = bf16[64,18,2048]{2,1,0:T(8,128)(2,1)S(1)} fusion(bf16[128,18,2048]{2,1,0:T(8,128)(2,1)} %all-to-all-done.2), kind=kLoop, calls=%fused_computation.9 | loop fusion | flops 2359296 | bytes 14155776 | tf_op jit(solution)/shard_map/reduce_sum | solution.py:140
  560.3 6.4 %copy_convert_fusion = f32[64,18,2048]{2,0,1:T(8,128)} fusion(bf16[64,18,2048]{2,1,0:T(8,128)(2,1)S(1)} %bitcast_reduce_fusion), kind=kLoop, calls=%fused_computation.18 | loop fusion | flops 2359296 | bytes 14155776 | tf_op jit(solution)/shard_map/convert_element_type | solution.py:142
  566.7 25.3 %gather_fusion.1 = f32[1024,2048]{1,0:T(8,128)} fusion(f32[64,18,2048]{2,0,1:T(8,128)} %copy_convert_fusion, s32[1024]{0:T(1024)S(1)} %bitcast.52), kind=kCustom, calls=%fused_computation.2 | custom fusion | bytes 16785408 | tf_op jit(solution)/shard_map/gather | solution.py:144
  592.0 6.6 %fusion.2 = f32[128,2048]{1,0:T(8,128)S(1)} fusion(f32[1024,2048]{1,0:T(8,128)} %gather_fusion.1, f32[128,8]{1,0:T(8,128)S(1)} %copy.102), kind=kLoop, calls=%fused_computation.11 | loop fusion | flops 3932160 | bytes 9441280 | tf_op jit(solution)/shard_map/reduce_sum | solution.py:145
  598.6 1.0 fusion.33
  (60 shorter events, 3.7 us)
Async XLA Ops:
  6.5 341.1 %copy-start = (bf16[1,512,2048]{2,1,0:T(8,128)(2,1)S(1)}, bf16[1,512,2048]{2,1,0:T(8,128)(2,1)}, u32[]{:S(2)}) copy-start(bf16[1,512,2048]{2,1,0:T(8,128)(2,1)} %param.27) | copy-start | bytes 6291460
  6.5 17.9 %copy-start.13 = (s32[16]{0:T(128)S(1)}, s32[16]{0:T(128)}, u32[]{:S(2)}) copy-start(s32[16]{0:T(128)} %param.23) | copy-start | bytes 196
  6.5 38.0 %all-gather.2.cloned.1.call-start = ((), (), s32[]{:S(2)}) async-start(), calls=%async_computation.4 | async-start | bytes 4718592 | tf_op jit(solution)/shard_map/all_gather | solution.py:57
  17.0 21.9 %all-to-all-start = ((bf16[16,64,2,256]{3,2,1,0:T(2,128)(2,1)}), bf16[16,64,2,256]{3,2,1,0:T(2,128)(2,1)S(1)}, u32[]{:S(2)}, u32[]{:S(2)}) async-start(bf16[16,64,2,256]{3,2,1,0:T(2,128)(2,1)} %broadcast_select_fusion), calls=%async_computation | async-start | bytes 2097152 | tf_op jit(solution)/shard_map/all_to_all | solution.py:71
  24.2 106.2 %reduce-scatter.2.cloned.1.call-start = ((), (), s32[]{:S(2)}) async-start(), calls=%async_computation.5 | async-start | bytes 4718592 | tf_op jit(solution)/shard_map/reduce_scatter | solution.py:104
  69.0 10.8 %copy-start.5 = (bf16[1024,1,256]{0,2,1:T(8,128)(2,1)S(1)}, bf16[1024,1,256]{0,2,1:T(8,128)(2,1)}, u32[]{:S(2)}) copy-start(bf16[1024,1,256]{0,2,1:T(8,128)(2,1)} %copy.86) | copy-start | bytes 1572868
  69.0 10.8 %copy-start.6 = (bf16[1024,256]{0,1:T(8,128)(2,1)S(1)}, bf16[1024,256]{0,1:T(8,128)(2,1)}, u32[]{:S(2)}) copy-start(bf16[1024,256]{0,1:T(8,128)(2,1)} %slice.68) | copy-start | bytes 1572868
  79.9 8.9 %copy-start.4 = (bf16[256,2048]{1,0:T(8,128)(2,1)S(1)}, bf16[256,2048]{1,0:T(8,128)(2,1)}, u32[]{:S(2)}) copy-start(bf16[256,2048]{1,0:T(8,128)(2,1)} %param.20) | copy-start | bytes 3145732
  88.7 3.3 copy-start.8
  92.0 19.1 %copy-start.11 = (s32[2]{0:T(128)S(1)}, s32[2]{0:T(128)}, u32[]{:S(2)}) copy-start(s32[2]{0:T(128)} %constant.94) | copy-start | bytes 28
  92.0 19.2 %copy-start.10 = (s32[2]{0:T(128)S(1)}, s32[2]{0:T(128)}, u32[]{:S(2)}) copy-start(s32[2]{0:T(128)} %constant.97) | copy-start | bytes 28
  92.0 38.4 %copy-start.1 = (bf16[128,2048]{1,0:T(8,128)(2,1)S(1)}, bf16[128,2048]{1,0:T(8,128)(2,1)}, u32[]{:S(2)}) copy-start(bf16[128,2048]{1,0:T(8,128)(2,1)} %param.15) | copy-start | bytes 1572868
  92.0 39.7 %copy-start.7 = (f32[2048]{0:T(1024)S(1)}, f32[2048]{0:T(1024)}, u32[]{:S(2)}) copy-start(f32[2048]{0:T(1024)} %param.24) | copy-start | bytes 24580
  327.0 8.6 %copy-start.2 = (bf16[2304,2048]{1,0:T(8,128)(2,1)S(1)}, bf16[2304,2048]{1,0:T(8,128)(2,1)}, u32[]{:S(2)}) copy-start(bf16[2304,2048]{1,0:T(8,128)(2,1)} %reshape.246) | copy-start | bytes 28311556
  327.0 8.6 %copy-start.12 = (bf16[1,2048,512]{2,1,0:T(8,128)(2,1)S(1)}, bf16[1,2048,512]{2,1,0:T(8,128)(2,1)}, u32[]{:S(2)}) copy-start(bf16[1,2048,512]{2,1,0:T(8,128)(2,1)} %param.26) | copy-start | bytes 6291460
  375.8 10.1 %copy-start.9 = (f32[128,8]{0,1:T(8,128)S(1)}, f32[128,8]{0,1:T(8,128)}, u32[]{:S(2)}) copy-start(f32[128,8]{0,1:T(8,128)} %param.29) | copy-start | bytes 12292
  375.8 175.6 %all-to-all-start.2 = ((bf16[128,18,2048]{2,1,0:T(8,128)(2,1)}), bf16[128,18,2048]{2,1,0:T(8,128)(2,1)}, u32[]{:S(2)}, u32[]{:S(2)}) async-start(bf16[128,18,2048]{2,1,0:T(8,128)(2,1)} %copy.100), calls=%async_computation.3 | async-start | bytes 25165824 | tf_op jit(solution)/shard_map/all_to_all | solution.py:132
  592.0 6.6 %copy-start.3 = (bf16[128,2048]{1,0:T(8,128)(2,1)S(1)}, bf16[128,2048]{1,0:T(8,128)(2,1)}, u32[]{:S(2)}) copy-start(bf16[128,2048]{1,0:T(8,128)(2,1)} %reduce-scatter.2.cloned.1.call-done) | copy-start | bytes 1572868
Sparse Core Ops, SparseCore 0:
  10.1 34.3 all-gather.1
  92.1 38.1 reduce-scatter.1
where the time goes:
time: 612 us; the launch traced here: 607 us
  waiting for transfers between devices  195 us (32%)
  blocking collectives  150 us (25%)
  local copies, waits for them, and re-layouts  118 us (19%)
  other arithmetic  58.9 us (10%)
  matrix products  52.5 us (9%)
  starting transfers between devices  17.5 us (3%)
  between operations  14 us (2%)
    all_to_all x1, waiting for transfers between devices, on_device(): lax.all_to_all(part.reshape(senders, count, width).astype(jnp.bfloat16),...  165 us
    all_to_all x1, blocking collectives, on_device(): lax.all_to_all(doubled, ('req', 'exp'), split_axis=0, concat_axis=0, tile...  150 us
    unnamed x35, local copies, waits for them, and re-layouts  31.7 us
    gather x1, local copies, waits for them, and re-layouts, on_device(): picked = combined[flat, slot].reshape(rows_dev, top_count, width)  25.3 us
    another operation x3, other arithmetic  21.9 us
    convert_element_type x1, local copies, waits for them, and re-layouts, on_device(): part.reshape(senders, count, width).astype(jnp.bfloat16)  20.9 us
    reduce_scatter x1, waiting for transfers between devices, on_device(): lax.psum_scatter(jnp.dot(attn, w_out, preferred_element_type=jnp.float32)...  19.1 us
    reshape x1, local copies, waits for them, and re-layouts, on_device(): joined_rows = rows_in.reshape(senders * count, width)  14.1 us
  transfers between devices with their start and end apart: 4, of which 4 were waited for; matrix products, arithmetic and copies ran while one was open for 6% of the time, Pallas kernels for 0%

commit v1 on v0

--- a/solution.py
+++ b/solution.py
@@ -6,6 +6,12 @@
 
 HD = 128
 PREFIX = 1024
+fill_circles = lambda payload, dim_at, where_dim: jnp.concatenate(
+    lax.all_to_all(
+        jnp.stack(jnp.split(payload, lax.psum(1, "req"), axis=where_dim), axis=0), "req", 0, 0
+    ),
+    axis=dim_at,
+)
 
 
 def norm_rows(values, gain):
@@ -68,7 +74,7 @@
         jnp.bfloat16
     )
     outgoing = jnp.take(prefix_cache, group_of, axis=0)
-    arrived = lax.all_to_all(outgoing, "req", split_axis=0, concat_axis=1, tiled=True)[0]
+    arrived = fill_circles(outgoing, 1, 0)[0]
     prefix_len = arrived.shape[0]
     query = projected[:, :local_width].reshape(slot_count, local_heads, head_dim)
     keys = jnp.concatenate(

time: 612 us -> 622 us (1.016)
  local copies, waits for them, and re-layouts: 118 us -> 129 us
    unnamed x35 -> x50, local copies, waits for them, and re-layouts: 31.7 us -> 41.7 us
  transfers between devices with their start and end apart: 4 -> 4, of which waited for: 4 -> 3; matrix products, arithmetic and copies ran while one was open for 6% -> 7% of each run, Pallas kernels for 0% -> 0%
where the time goes in v1:
time: 622 us; the launch traced here: 616 us
  waiting for transfers between devices  195 us (31%)
  blocking collectives  150 us (24%)
  local copies, waits for them, and re-layouts  129 us (21%)
  other arithmetic  57.9 us (9%)
  matrix products  52.5 us (8%)
  starting transfers between devices  17.5 us (3%)
  between operations  14 us (2%)
    all_to_all x1, waiting for transfers between devices, on_device(): lax.all_to_all(part.reshape(senders, count, width).astype(jnp.bfloat16),...  165 us
    all_to_all x1, blocking collectives, on_device(): lax.all_to_all(doubled, ('req', 'exp'), split_axis=0, concat_axis=0, tile...  150 us
    unnamed x50, local copies, waits for them, and re-layouts  41.7 us
    gather x1, local copies, waits for them, and re-layouts, on_device(): picked = combined[flat, slot].reshape(rows_dev, top_count, width)  25.3 us
    another operation x3, other arithmetic  21.9 us
    convert_element_type x1, local copies, waits for them, and re-layouts, on_device(): part.reshape(senders, count, width).astype(jnp.bfloat16)  20.9 us
    reduce_scatter x1, waiting for transfers between devices, on_device(): lax.psum_scatter(jnp.dot(attn, w_out, preferred_element_type=jnp.float32)...  20.3 us
    reshape x1, local copies, waits for them, and re-layouts, on_device(): joined_rows = rows_in.reshape(senders * count, width)  14.1 us
  transfers between devices with their start and end apart: 4, of which 3 were waited for; matrix products, arithmetic and copies ran while one was open for 7% of the time, Pallas kernels for 0%

profile of v1, /device:TPU:24, one launch (start us, length us, event | category | flops | bytes accessed | tf_op | source)
XLA Modules:
  0.0 616.3 jit_solution(3637615925226559148)
XLA Ops:
  6.5 1.4 fusion.25
  7.9 2.0 fusion.27
  10.7 3.7 gather_fusion
  14.4 0.7 compare_and_fusion
  15.0 1.0 broadcast_select_fusion
  16.0 0.7 fusion.56
  19.3 0.7 fusion.51
  26.6 7.2 %all-to-all-start = ((bf16[16,1,64,2,256]{4,3,2,1,0:T(2,128)(2,1)}), bf16[16,1,64,2,256]{4,3,2,1,0:T(2,128)(2,1)S(1)}, u32[]{:S(2)}, u32[]{:S(2)}) async-start(bf16[16,1,64,2,256]{4,3,2,1,0:T(2,128)(2,1)} %fusion.41), calls=%async_computation | async-start | bytes 2097152 | tf_op jit(solution)/shard_map/all_to_all | solution.py:10
  35.4 3.1 multiply_cosine_fusion
  38.4 10.1 %all-to-all-done = bf16[16,1,64,2,256]{4,3,2,1,0:T(2,128)(2,1)S(1)} async-done(((bf16[16,1,64,2,256]{4,3,2,1,0:T(2,128)(2,1)}), bf16[16,1,64,2,256]{4,3,2,1,0:T(2,128)(2,1)S(1)}, u32[]{:S(2)}, u32[]{:S(2)}) %all-to-all-start) | async-done | bytes 1048608 | tf_op jit(solution)/shard_map/all_to_all | solution.py:10
  48.8 0.9 fusion.66
  49.6 1.2 copy.104
  50.9 1.0 copy.107
  51.9 1.0 copy.101
  52.9 6.7 %fusion.10 = f32[1024,768]{0,1:T(8,128)S(1)} fusion(bf16[1024,2048]{1,0:T(8,128)(2,1)} %all-gather.2.cloned.1.call-done, bf16[2048,256]{1,0:T(8,128)(2,1)} %param.19, bf16[2048,256]{1,0:T(8,128)(2,1)} %param.18, bf16[2048,256]{1,0:T(8,128)(2,1)} %param.17), kind=kOutput, calls=%fused_computation.23 | convolution fusion | flops 3230662656 | bytes 10485760 | tf_op jit(solution)/shard_map/dot_general | solution.py:65
  59.6 1.2 fusion.65
  60.8 0.9 slice.68
  61.7 1.0 fusion.67
  62.7 1.4 copy.118
  64.1 2.4 copy.119
  66.5 2.3 fusion.68
  68.8 2.4 copy.120
  71.1 2.4 copy.121
  73.5 3.9 subtract_convert_fusion.1
  77.4 10.8 %fusion.69 = (f32[2,1024]{1,0:T(2,128)S(1)}, f32[2,1024,2048]{2,1,0:T(8,128)}) fusion(pred[2048]{0:T(1024)(128)(4,1)S(1)} %concatenate.28, bf16[1024,2,64]{2,0,1:T(8,128)(2,1)} %get-tuple-element.13, bf16[1024,2,64]{2,0,1:T(8,128)(2,1)} %get-tuple-element.14, bf16[1024,2,128]{2,0,1:T(8,128)(2,1)} %copy.107, bf16[1024,2,64]{2,0,1:T(8,128)(2,1)} %get-tuple-element.6, ...), kind=kOutput, calls=%fused_computation.137 | convolution fusion | flops 1094715392 | bytes 18360320 | tf_op jit(solution)/shard_map/sub | solution.py:103
  88.3 8.8 %fusion.24 = bf16[2,128,1024]{2,1,0:T(8,128)(2,1)S(1)} fusion(f32[2,1024,2048]{2,1,0:T(8,128)} %get-tuple-element.25, f32[2,1024]{1,0:T(2,128)S(1)} %get-tuple-element.24, bf16[1024,2,128]{0,2,1:T(8,128)(2,1)S(1)} %bitcast.126, bf16[1024,2,128]{0,2,1:T(8,128)(2,1)S(1)} %bitcast.125), kind=kOutput, calls=%fused_computation.43 | convolution fusion | flops 1084489728 | bytes 18358272 | tf_op jit(solution)/shard_map/hqk,khd->qhd/dot_general | solution.py:106
  97.1 3.2 convolution_convert_fusion.1
  100.8 18.0 %reduce-window.6 = s32[64,8,128]{2,1,0:T(8,128)S(1)} reduce-window(s32[64,8,128]{2,1,0:T(8,128)S(1)} %fusion.39, s32[]{:T(128)} %constant.39.clone.1), window={size=1x1x128 pad=0_0x0_0x127_0}, to_apply=%region_4.5 | reduce-window | flops 8323072 | bytes 524292 | tf_op jit(solution)/shard_map/reduce-window
  119.7 20.3 %reduce-scatter.2.cloned.1.call-done = bf16[128,2048]{1,0:T(8,128)(2,1)} async-done(((bf16[1024,2048]{1,0:T(8,128)(2,1)}), bf16[128,2048]{1,0:T(8,128)(2,1)}) %reduce-scatter.2.cloned.1.call-update) | async-done | bytes 524304 | tf_op jit(solution)/shard_map/reduce_scatter | solution.py:110
  140.0 1.3 fusion.29
  141.3 1.3 fusion.31
  142.6 23.0 %scatter_custom_fusion = bf16[1152,2048]{1,0:T(8,128)(2,1)} fusion(s32[1024]{0:T(1024)S(1)} %get-tuple-element.27, bf16[128,2048]{1,0:T(8,128)(2,1)S(1)} %fusion.31, s32[1024]{0:T(1024)S(1)} %get-tuple-element.26, bf16[]{:T(256)} %constant.82.clone.1), kind=kCustom, calls=%fused_computation.20 | custom fusion | bytes 4718594
  165.6 5.1 copy.113
  170.6 1.6 broadcast_in_dim.43
  172.2 150.4 %all_to_all.15 = bf16[128,18,2048]{2,1,0:T(8,128)(2,1)} all-to-all(bf16[128,18,2048]{2,1,0:T(8,128)(2,1)S(1)} %bitcast.117), channel_id=1, replica_groups=mesh['req'=16,'exp'=8] {'req','exp'}, dimensions={0} | all-to-all | bytes 18874368 | tf_op jit(solution)/shard_map/all_to_all | solution.py:131
  322.6 14.1 %reshape.242 = bf16[2304,2048]{1,0:T(8,128)(2,1)} reshape(bf16[128,18,2048]{2,1,0:T(8,128)(2,1)} %all_to_all.15) | data formatting | bytes 18874368 | tf_op jit(solution)/shard_map/reshape | solution.py:133
  336.7 8.6 %fusion.20 = f32[2304,512]{1,0:T(8,128)S(1)} fusion(bf16[2304,2048]{1,0:T(8,128)(2,1)} %reshape.242, bf16[1,2048,512]{2,1,0:T(8,128)(2,1)} %param.25), kind=kOutput, calls=%fused_computation.33 | convolution fusion | flops 4831838208 | bytes 16252928 | tf_op jit(solution)/shard_map/dot_general | solution.py:134
  345.3 7.1 %fusion.7 = bf16[2304,512]{1,0:T(8,128)(2,1)} fusion(bf16[2304,2048]{1,0:T(8,128)(2,1)S(1)} %copy-done.2, f32[2304,512]{1,0:T(8,128)S(1)} %fusion.20, bf16[1,2048,512]{2,1,0:T(8,128)(2,1)S(1)} %copy-done.12), kind=kOutput, calls=%fused_computation.19 | convolution fusion | flops 4838916096 | bytes 18612224 | tf_op jit(solution)/shard_map/dot_general | solution.py:135
  352.4 4.9 dot_general.29
  357.2 7.3 %convolution_convert_fusion = bf16[128,18,2048]{2,0,1:T(8,128)(2,1)S(1)} fusion(bf16[128,18,512]{2,1,0:T(8,128)(2,1)} %dot_general.29, bf16[1,512,2048]{2,1,0:T(8,128)(2,1)S(1)} %copy-done), kind=kOutput, calls=%fused_computation.16 | convolution fusion | flops 4836556800 | bytes 13893632 | tf_op jit(solution)/shard_map/dot_general | solution.py:137
  364.5 20.9 %copy.115 = bf16[128,18,2048]{2,1,0:T(8,128)(2,1)} copy(bf16[128,18,2048]{2,0,1:T(8,128)(2,1)S(1)} %convolution_convert_fusion) | data formatting | bytes 18874368 | tf_op jit(solution)/shard_map/convert_element_type | solution.py:139
  385.5 10.1 %all-to-all-start.2 = ((bf16[128,18,2048]{2,1,0:T(8,128)(2,1)}), bf16[128,18,2048]{2,1,0:T(8,128)(2,1)}, u32[]{:S(2)}, u32[]{:S(2)}) async-start(bf16[128,18,2048]{2,1,0:T(8,128)(2,1)} %copy.115), calls=%async_computation.3 | async-start | bytes 25165824 | tf_op jit(solution)/shard_map/all_to_all | solution.py:138
  396.3 164.7 %all-to-all-done.2 = bf16[128,18,2048]{2,1,0:T(8,128)(2,1)} async-done(((bf16[128,18,2048]{2,1,0:T(8,128)(2,1)}), bf16[128,18,2048]{2,1,0:T(8,128)(2,1)}, u32[]{:S(2)}, u32[]{:S(2)}) %all-to-all-start.2) | async-done | bytes 9437216 | tf_op jit(solution)/shard_map/all_to_all | solution.py:138
  561.0 8.9 %bitcast_reduce_fusion = bf16[64,18,2048]{2,1,0:T(8,128)(2,1)S(1)} fusion(bf16[128,18,2048]{2,1,0:T(8,128)(2,1)} %all-to-all-done.2), kind=kLoop, calls=%fused_computation.9 | loop fusion | flops 2359296 | bytes 14155776 | tf_op jit(solution)/shard_map/reduce_sum | solution.py:146
  569.9 6.4 %copy_convert_fusion = f32[64,18,2048]{2,0,1:T(8,128)} fusion(bf16[64,18,2048]{2,1,0:T(8,128)(2,1)S(1)} %bitcast_reduce_fusion), kind=kLoop, calls=%fused_computation.18 | loop fusion | flops 2359296 | bytes 14155776 | tf_op jit(solution)/shard_map/convert_element_type | solution.py:148
  576.3 25.3 %gather_fusion.1 = f32[1024,2048]{1,0:T(8,128)} fusion(f32[64,18,2048]{2,0,1:T(8,128)} %copy_convert_fusion, s32[1024]{0:T(1024)S(1)} %bitcast.116), kind=kCustom, calls=%fused_computation.2 | custom fusion | bytes 16785408 | tf_op jit(solution)/shard_map/gather | solution.py:150
  601.6 6.6 %fusion.2 = f32[128,2048]{1,0:T(8,128)S(1)} fusion(f32[1024,2048]{1,0:T(8,128)} %gather_fusion.1, f32[128,8]{1,0:T(8,128)S(1)} %copy.117), kind=kLoop, calls=%fused_computation.11 | loop fusion | flops 3932160 | bytes 9441280 | tf_op jit(solution)/shard_map/reduce_sum | solution.py:151
  608.2 1.0 fusion.33
  (76 shorter events, 13.7 us)
Async XLA Ops:
  6.5 350.7 %copy-start = (bf16[1,512,2048]{2,1,0:T(8,128)(2,1)S(1)}, bf16[1,512,2048]{2,1,0:T(8,128)(2,1)}, u32[]{:S(2)}) copy-start(bf16[1,512,2048]{2,1,0:T(8,128)(2,1)} %param.27) | copy-start | bytes 6291460
  6.5 46.4 %all-gather.2.cloned.1.call-start = ((), (), s32[]{:S(2)}) async-start(), calls=%async_computation.4 | async-start | bytes 4718592 | tf_op jit(solution)/shard_map/all_gather | solution.py:63
  10.0 24.1 %copy-start.13 = (s32[16]{0:T(128)S(1)}, s32[16]{0:T(128)}, u32[]{:S(2)}) copy-start(s32[16]{0:T(128)} %param.23) | copy-start | bytes 196
  26.6 21.9 %all-to-all-start = ((bf16[16,1,64,2,256]{4,3,2,1,0:T(2,128)(2,1)}), bf16[16,1,64,2,256]{4,3,2,1,0:T(2,128)(2,1)S(1)}, u32[]{:S(2)}, u32[]{:S(2)}) async-start(bf16[16,1,64,2,256]{4,3,2,1,0:T(2,128)(2,1)} %fusion.41), calls=%async_computation | async-start | bytes 2097152 | tf_op jit(solution)/shard_map/all_to_all | solution.py:10
  33.8 106.2 %reduce-scatter.2.cloned.1.call-start = ((), (), s32[]{:S(2)}) async-start(), calls=%async_computation.5 | async-start | bytes 4718592 | tf_op jit(solution)/shard_map/reduce_scatter | solution.py:110
  77.4 10.8 %copy-start.5 = (bf16[1024,1,256]{0,2,1:T(8,128)(2,1)S(1)}, bf16[1024,1,256]{0,2,1:T(8,128)(2,1)}, u32[]{:S(2)}) copy-start(bf16[1024,1,256]{0,2,1:T(8,128)(2,1)} %copy.101) | copy-start | bytes 1572868
  77.4 10.8 %copy-start.6 = (bf16[1024,256]{0,1:T(8,128)(2,1)S(1)}, bf16[1024,256]{0,1:T(8,128)(2,1)}, u32[]{:S(2)}) copy-start(bf16[1024,256]{0,1:T(8,128)(2,1)} %slice.68) | copy-start | bytes 1572868
  88.3 8.9 %copy-start.4 = (bf16[256,2048]{1,0:T(8,128)(2,1)S(1)}, bf16[256,2048]{1,0:T(8,128)(2,1)}, u32[]{:S(2)}) copy-start(bf16[256,2048]{1,0:T(8,128)(2,1)} %param.20) | copy-start | bytes 3145732
  97.1 3.3 copy-start.8
  100.4 19.1 %copy-start.11 = (s32[2]{0:T(128)S(1)}, s32[2]{0:T(128)}, u32[]{:S(2)}) copy-start(s32[2]{0:T(128)} %constant.94) | copy-start | bytes 28
  100.4 19.2 %copy-start.10 = (s32[2]{0:T(128)S(1)}, s32[2]{0:T(128)}, u32[]{:S(2)}) copy-start(s32[2]{0:T(128)} %constant.97) | copy-start | bytes 28
  100.4 39.6 %copy-start.1 = (bf16[128,2048]{1,0:T(8,128)(2,1)S(1)}, bf16[128,2048]{1,0:T(8,128)(2,1)}, u32[]{:S(2)}) copy-start(bf16[128,2048]{1,0:T(8,128)(2,1)} %param.15) | copy-start | bytes 1572868
  100.4 41.0 %copy-start.7 = (f32[2048]{0:T(1024)S(1)}, f32[2048]{0:T(1024)}, u32[]{:S(2)}) copy-start(f32[2048]{0:T(1024)} %param.24) | copy-start | bytes 24580
  336.7 8.6 %copy-start.2 = (bf16[2304,2048]{1,0:T(8,128)(2,1)S(1)}, bf16[2304,2048]{1,0:T(8,128)(2,1)}, u32[]{:S(2)}) copy-start(bf16[2304,2048]{1,0:T(8,128)(2,1)} %reshape.242) | copy-start | bytes 28311556
  336.7 8.6 %copy-start.12 = (bf16[1,2048,512]{2,1,0:T(8,128)(2,1)S(1)}, bf16[1,2048,512]{2,1,0:T(8,128)(2,1)}, u32[]{:S(2)}) copy-start(bf16[1,2048,512]{2,1,0:T(8,128)(2,1)} %param.26) | copy-start | bytes 6291460
  385.5 10.1 %copy-start.9 = (f32[128,8]{0,1:T(8,128)S(1)}, f32[128,8]{0,1:T(8,128)}, u32[]{:S(2)}) copy-start(f32[128,8]{0,1:T(8,128)} %param.29) | copy-start | bytes 12292
  385.5 175.6 %all-to-all-start.2 = ((bf16[128,18,2048]{2,1,0:T(8,128)(2,1)}), bf16[128,18,2048]{2,1,0:T(8,128)(2,1)}, u32[]{:S(2)}, u32[]{:S(2)}) async-start(bf16[128,18,2048]{2,1,0:T(8,128)(2,1)} %copy.115), calls=%async_computation.3 | async-start | bytes 25165824 | tf_op jit(solution)/shard_map/all_to_all | solution.py:138
  601.6 6.6 %copy-start.3 = (bf16[128,2048]{1,0:T(8,128)(2,1)S(1)}, bf16[128,2048]{1,0:T(8,128)(2,1)}, u32[]{:S(2)}) copy-start(bf16[128,2048]{1,0:T(8,128)(2,1)} %reduce-scatter.2.cloned.1.call-done) | copy-start | bytes 1572868
Sparse Core Ops, SparseCore 0:
  10.1 34.3 all-gather.1
  100.5 39.4 reduce-scatter.1
